TPU v7x, 128 devices: a whole 4x4x4 slice. The times are simulated.
128 devices in a mesh: blk: 32 (over x, y, core), mp: 4 (over z).
Axes of the slice: x: 4, y: 4, z: 4, core: 2. Of those that a mesh axis runs over, the one named last changes fastest.
Arguments:
- hidden: bfloat16 [144, 3584], replicated, may hold values from -6 to 6
- medusa_w: bfloat16 [2, 3584, 3584], P(None, 'blk', 'mp'), may hold values from -0.09375 to 0.09375
- embedding: bfloat16 [131072, 3584], P(('blk', 'mp')), may hold values from -0.5 to 0.5
- cand_ids: int32 [2, 144, 10], replicated, may hold values from 0 to 131071
- tree_q: bfloat16 [12, 48, 4096], P(None, None, 'mp'), may hold values from -6 to 6
- tree_key_value: bfloat16 [2, 12, 48, 2048], P(None, None, None, 'mp'), may hold values from -6 to 6
- prompt_key_value: bfloat16 [2, 32, 2048, 2048], P(None, 'blk', None, 'mp'), may hold values from -6 to 6
- block_group: int32 [32], P('blk'), may hold values from 0 to 11, as said below
- block_len: int32 [32], P('blk'), may hold values from 1 to 2048
- block_empty: int32 [32], P('blk'), may hold values 0 or 1
- parents: int32 [12, 48], replicated, may hold values from 0 to 46, as said below
- out_weight: bfloat16 [4096, 3584], P('mp'), may hold values from -0.09375 to 0.09375
- post_gain: float32 [3584], replicated, may hold values from 0.5 to 1.5
- resid: bfloat16 [576, 3584], P('blk'), may hold values from -6 to 6
Outputs:
- draft_logprob: float32 [2, 144, 10], replicated
- layer_out: bfloat16 [576, 3584], P('blk')
Inputs may be any that keep to these rules, and one draw needn't show every extreme that they name: `block_group`: every group number from 0 to min(12, 32) - 1 owns at least one block. `parents`: entry 0 of each row is 0; entry i for i >= 1 is below i; some group's last token has parent 48 - 2.
All inputs are finite; a program needn't handle non-finite values. No bound on the sum of `block_empty` on one device may be relied on, other than what follows from the above.
Results may differ from a plain program's by a relative error of at most 0.005.
Values may be sent and summed in bfloat16 or wider, within the bound.
A program may use at most 128 MiB of HBM per device.

v0:
```python
import jax
import jax.numpy as jnp
from jax import lax
from jax.sharding import PartitionSpec as P

HEAD_SIZE = 256


def capped(values, limit):
    return limit * jnp.tanh(values / limit)


def ancestry(parents):
    count = parents.shape[1]
    column = jnp.arange(count, dtype=jnp.int32)
    linked = (parents[:, :, None] == column[None, None, :]) & (column[None, :, None] > 0)
    reach = jnp.eye(count, dtype=jnp.float32)[None] + linked.astype(jnp.float32)
    for sweep in range(count.bit_length()):
        reach = jnp.minimum(
            jnp.einsum("gij,gjk->gik", reach, reach, precision=lax.Precision.HIGHEST), 1.0
        )
    return reach


def attend(queries, keys, values, mask):
    rows = queries.shape[0]
    length = keys.shape[0]
    kv_heads = keys.shape[1] // HEAD_SIZE
    repeats = queries.shape[1] // keys.shape[1]
    query_view = queries.reshape(rows, kv_heads, repeats, HEAD_SIZE)
    key_view = keys.reshape(length, kv_heads, HEAD_SIZE)
    value_view = values.reshape(length, kv_heads, HEAD_SIZE)
    scores = jnp.einsum(
        "qhrd,khd->hrqk", query_view, key_view, preferred_element_type=jnp.float32
    ) * HEAD_SIZE ** (-0.5)
    weights = jnp.exp(capped(scores, 50.0)) * mask[None, None]
    denominator = jnp.sum(weights, -1).transpose(2, 0, 1).reshape(rows, kv_heads * repeats)
    numerator = jnp.einsum(
        "hrqk,khd->qhrd",
        weights.astype(jnp.bfloat16),
        value_view,
        preferred_element_type=jnp.float32,
    )
    return (numerator.reshape(rows, kv_heads * repeats * HEAD_SIZE), denominator)


def per_device(
    hidden,
    medusa_w,
    embedding,
    cand_ids,
    tree_q,
    tree_key_value,
    prompt_key_value,
    block_group,
    block_len,
    block_empty,
    parents,
    out_weight,
    post_gain,
    resid,
):
    units = medusa_w.shape[2]
    inner = jnp.einsum(
        "rd,mdu->mru",
        hidden,
        lax.all_gather(medusa_w, "blk", axis=1, tiled=True),
        preferred_element_type=jnp.float32,
    )
    own_cols = lax.dynamic_slice_in_dim(hidden, lax.axis_index("mp") * units, units, 1).astype(
        jnp.float32
    )
    fresh = (own_cols[None] + jax.nn.silu(inner)).astype(jnp.bfloat16)
    full_fresh = lax.all_gather(fresh, "mp", axis=2, tiled=True)
    logits = capped(
        jnp.einsum("mrd,vd->mrv", full_fresh, embedding, preferred_element_type=jnp.float32), 30.0
    )
    totals = jnp.sum(jnp.exp(logits), -1)
    vocab_dev = embedding.shape[0]
    first_id = lax.axis_index(("blk", "mp")) * vocab_dev
    local_ids = cand_ids - first_id
    match = local_ids[..., None] == jnp.arange(vocab_dev, dtype=jnp.int32)
    picked = jnp.sum(jnp.where(match, logits[:, :, None, :], 0.0), -1)
    totals, picked = lax.psum((totals, picked), ("blk", "mp"))
    draft_logprob = picked - jnp.log(totals)[..., None]
    groups, tree_size, features = tree_q.shape
    keys = prompt_key_value[0, 0]
    values = prompt_key_value[1, 0]
    length = keys.shape[0]
    group = block_group[0]
    key_ok = ((jnp.arange(length, dtype=jnp.int32) < block_len[0]) & (block_empty[0] == 0)).astype(
        jnp.float32
    )
    row_group = jnp.arange(groups * tree_size, dtype=jnp.int32) // tree_size
    mask = (row_group == group).astype(jnp.float32)[:, None] * key_ok[None, :]
    numer, denom = attend(tree_q.reshape(groups * tree_size, features), keys, values, mask)
    rows_dev = groups * tree_size // lax.axis_size("blk")
    first_row = lax.axis_index("blk") * rows_dev
    summed = lax.psum((numer, denom), "blk")
    numer = lax.dynamic_slice_in_dim(summed[0], first_row, rows_dev, 0)
    denom = lax.dynamic_slice_in_dim(summed[1], first_row, rows_dev, 0)
    reach = ancestry(parents)
    tree_numer, tree_denom = jax.vmap(attend)(tree_q, tree_key_value[0], tree_key_value[1], reach)
    heads_dev = tree_denom.shape[2]
    tree_numer = lax.dynamic_slice_in_dim(
        tree_numer.reshape(groups * tree_size, features), first_row, rows_dev, 0
    )
    tree_denom = lax.dynamic_slice_in_dim(
        tree_denom.reshape(groups * tree_size, heads_dev), first_row, rows_dev, 0
    )
    numer = numer + tree_numer
    denom = denom + tree_denom
    heads_out = (
        (numer.reshape(rows_dev, heads_dev, HEAD_SIZE) / denom[..., None])
        .reshape(rows_dev, features)
        .astype(jnp.bfloat16)
    )
    attn = lax.psum(jnp.dot(heads_out, out_weight, preferred_element_type=jnp.float32), "mp")
    normed = attn * lax.rsqrt(jnp.mean(attn * attn, -1, keepdims=True) + 1e-06) * post_gain
    layer_out = (normed + resid.astype(jnp.float32)).astype(jnp.bfloat16)
    return (draft_logprob, layer_out)


def solution(mesh):
    placed = (
        P(),
        P(None, "blk", "mp"),
        P(("blk", "mp"), None),
        P(),
        P(None, None, "mp"),
        P(None, None, None, "mp"),
        P(None, "blk", None, "mp"),
        P("blk"),
        P("blk"),
        P("blk"),
        P(),
        P("mp", None),
        P(),
        P("blk", None),
    )
    return jax.shard_map(
        per_device, mesh=mesh, in_specs=placed, out_specs=(P(), P("blk", None)), check_vma=False
    )
```

profile of v0, /device:TPU:1, one launch (start us, length us, event | category | flops | bytes accessed | tf_op | source)
XLA Modules:
  0.0 381.7 jit_solution(4261685247920140671)
XLA Ops:
  7.2 0.0 all-reduce.4.cloned.1.call-start
  7.2 4.4 %fusion.51 = (bf16[1,1,2048,512]{3,2,1,0:T(8,128)(2,1)}, bf16[1,1,2048,512]{3,2,1,0:T(8,128)(2,1)}) fusion(bf16[2,1,2048,512]{3,2,1,0:T(8,128)(2,1)} %param.20), kind=kLoop, calls=%fused_computation.70 | loop fusion | bytes 8388608 | tf_op jit(solution)/shard_map/slice | solution.py:88
  11.6 2.9 copy.79
  16.5 3.3 reshape_reshape.3
  19.8 4.0 %copy.80 = bf16[1,1,2048,512]{2,3,1,0:T(8,128)(2,1)} copy(bf16[1,1,2048,512]{3,2,1,0:T(8,128)(2,1)} %get-tuple-element.6) | data formatting | bytes 4194304
  23.8 0.4 broadcast_multiply_fusion
  24.2 10.5 %fusion = (f32[2,2,576]{2,1,0:T(2,128)}, f32[2,2048,576,2]{1,2,3,0:T(8,128)}) fusion(f32[576,2048]{1,0:T(8,128)S(1)} %broadcast_multiply_fusion, bf16[2048,2,256,1]{0,2,3,1:T(8,128)(2,1)S(1)} %bitcast.83, bf16[576,2,2,256]{3,2,1,0:T(2,128)(2,1)S(1)} %reshape_reshape.3), kind=kOutput, calls=%fused_computation.1 | convolution fusion | flops 2434791168 | bytes 26878976 | tf_op jit(solution)/shard_map/qhrd,khd->hrqk/dot_general | solution.py:33
  34.7 9.1 %fusion.6 = f32[576,2,2,256]{3,0,2,1:T(8,128)S(1)} fusion(bf16[2048,2,256,1]{0,2,3,1:T(8,128)(2,1)S(1)} %bitcast.85, f32[2,2048,576,2]{1,2,3,0:T(8,128)} %get-tuple-element.15, f32[576,2048]{1,0:T(8,128)S(1)} %broadcast_multiply_fusion), kind=kOutput, calls=%fused_computation.10 | convolution fusion | flops 2434793472 | bytes 28049408 | tf_op jit(solution)/shard_map/hrqk,khd->qhrd/dot_general | solution.py:38
  43.8 1.8 copy.56
  45.6 2.9 reshape.101
  48.6 0.0 all-gather.3.cloned.1.call-start
  48.6 0.7 all-gather.3.cloned.1.call-update
  49.3 0.2 all-reduce.6.cloned.1.call-start
  49.6 0.3 copy-done
  49.8 0.9 reshape.102
  50.7 0.7 reshape.104
  51.4 0.1 fusion.52
  51.5 0.1 reshape_squeeze.14
  51.7 1.4 convolution_minimum_fusion.5
  53.1 0.4 convolution_minimum_fusion.4
  53.5 0.4 convolution_minimum_fusion.3
  53.9 0.4 convolution_minimum_fusion.2
  54.4 0.4 convolution_minimum_fusion.1
  54.8 0.4 convolution_minimum_fusion
  55.2 0.1 copy.59
  55.3 0.9 fusion.53
  56.2 0.1 reshape.105
  56.3 124.9 %psum.38 = f32[576,4]{0,1:T(4,128)S(1)} all-reduce(f32[576,4]{0,1:T(4,128)S(1)} %reshape.104), channel_id=1, replica_groups=mesh['blk'=32,'mp'=4] {'blk'}, use_global_device_ids=true, to_apply=%region_6.7 | all-reduce | flops 2304 | bytes 18432 | tf_op jit(solution)/shard_map/psum | solution.py:99
  181.2 0.1 dynamic-slice_add_fusion
  181.3 0.1 copy.64
  181.4 0.1 div.48
  181.5 0.1 reshape_squeeze.15
  181.7 0.5 convolution_bitcast_fusion
  182.2 1.8 copy.62
  184.1 2.9 reshape.103
  187.0 0.0 all-reduce.4.cloned.1.call-done
  187.1 5.1 %fusion.39 = f32[18,3584]{1,0:T(8,128)} fusion(bf16[1024,3584]{1,0:T(8,128)(2,1)} %param.25, f32[18,1024]{1,0:T(8,128)S(1)} %bitcast.87, f32[576,1024]{1,0:T(8,128)} %reshape.103, s32[]{:T(128)S(6)} %select_n.25, f32[576,1024]{1,0:T(8,128)} %all-reduce.4.cloned.1.call-done), kind=kOutput, calls=%fused_computation.47 | convolution fusion | flops 132175872 | bytes 7868420 | tf_op jit(solution)/shard_map/dot_general | solution.py:118
  192.2 0.3 all-gather.5.cloned.1.call-start
  192.4 32.7 %all-gather.3.cloned.1.call-done = bf16[2,3584,896]{2,1,0:T(8,128)(2,1)} async-done(((bf16[2,112,896]{2,1,0:T(8,128)(2,1)}), bf16[2,3584,896]{2,1,0:T(8,128)(2,1)}) %all-gather.3.cloned.1.call-update) | async-done | bytes 12845072 | tf_op jit(solution)/shard_map/all_gather | solution.py:67
  225.2 7.6 %add_convert_fusion = bf16[2,144,896]{2,1,0:T(8,128)(2,1)} fusion(bf16[2,3584,896]{2,1,0:T(8,128)(2,1)} %all-gather.3.cloned.1.call-done, bf16[144,3584]{1,0:T(8,128)(2,1)S(1)} %copy-done.4, f32[144,896]{1,0:T(8,128)S(1)} %dynamic-slice_convert_fusion), kind=kOutput, calls=%fused_computation.32 | convolution fusion | flops 1851236352 | bytes 14909440 | tf_op jit(solution)/shard_map/rd,mdu->mru/dot_general | solution.py:64
  232.8 34.1 %all-reduce.6.cloned.1.call-done = f32[18,3584]{1,0:T(8,128)} async-done(((f32[18,3584]{1,0:T(8,128)}), f32[18,3584]{1,0:T(8,128)}) %all-reduce.6.cloned.1.call-update) | async-done | bytes 258064 | tf_op jit(solution)/shard_map/psum | solution.py:118
  266.9 1.1 multiply_reduce_fusion
  268.0 1.8 add_convert_fusion.1
  269.8 31.7 %all-gather.5.cloned.1.call-done = bf16[2,144,3584]{2,1,0:T(8,128)(2,1)} async-done(((bf16[2,144,896]{2,1,0:T(8,128)(2,1)}), bf16[2,144,3584]{2,1,0:T(8,128)(2,1)}) %all-gather.5.cloned.1.call-update) | async-done | bytes 2064400 | tf_op jit(solution)/shard_map/all_gather | solution.py:74
  301.5 6.2 %exponential_reduce_fusion = (f32[2,144]{1,0:T(2,128)S(1)}, f32[2,144,1024]{2,1,0:T(8,128)S(1)}) fusion(bf16[2,144,3584]{2,1,0:T(8,128)(2,1)} %all-gather.5.cloned.1.call-done, bf16[1024,3584]{1,0:T(8,128)(2,1)} %param.16), kind=kOutput, calls=%fused_computation.24 | convolution fusion | flops 2114813696 | bytes 10585216 | tf_op jit(solution)/shard_map/mrd,vd->mrv/dot_general | solution.py:76
  307.8 1.8 select_reduce_fusion
  309.6 64.9 %all-reduce = (f32[2,144,10]{1,2,0:T(8,128)S(1)}, f32[2,144]{1,0:T(2,128)S(1)}) all-reduce(f32[2,144,10]{1,2,0:T(8,128)S(1)} %select_reduce_fusion, f32[2,144]{1,0:T(2,128)S(1)} %get-tuple-element.10), channel_id=1, replica_groups=mesh['blk'=32,'mp'=4] {'blk','mp'}, use_global_device_ids=true, to_apply=%region_1.2 | all-reduce | flops 3168 | bytes 25344 | tf_op jit(solution)/shard_map/psum | solution.py:84
  374.5 0.6 copy.65
  (29 shorter events, 0.2 us)
Async XLA Ops:
  7.2 179.9 %all-reduce.4.cloned.1.call-start = ((), (), s32[]{:S(2)}) async-start(), calls=%async_computation.2 | async-start | bytes 4718592 | tf_op jit(solution)/shard_map/psum | solution.py:99
  24.2 10.5 %copy-start.1 = (bf16[1,1,2048,512]{2,3,1,0:T(8,128)(2,1)S(1)}, bf16[1,1,2048,512]{2,3,1,0:T(8,128)(2,1)}, u32[]{:S(2)}) copy-start(bf16[1,1,2048,512]{2,3,1,0:T(8,128)(2,1)} %copy.80) | copy-start | bytes 6291460
  48.6 1.3 copy-start
  48.6 2.9 copy-start.2
  48.6 176.6 %all-gather.3.cloned.1.call-start = ((), (), s32[]{:S(2)}) async-start(), calls=%async_computation | async-start | bytes 13246464 | tf_op jit(solution)/shard_map/all_gather | solution.py:67
  49.3 217.6 %all-reduce.6.cloned.1.call-start = ((), (), s32[]{:S(2)}) async-start(), calls=%async_computation.3 | async-start | bytes 688128 | tf_op jit(solution)/shard_map/psum | solution.py:118
  184.0 3.0 copy-start.4
  192.1 40.7 %copy-start.5 = (s32[2,144,10]{1,0,2:T(2,128)S(1)}, s32[2,144,10]{1,0,2:T(2,128)}, u32[]{:S(2)}) copy-start(s32[2,144,10]{1,0,2:T(2,128)} %param.17) | copy-start | bytes 34564
  192.2 75.9 %copy-start.3 = (bf16[18,3584]{1,0:T(8,128)(2,1)S(1)}, bf16[18,3584]{1,0:T(8,128)(2,1)}, u32[]{:S(2)}) copy-start(bf16[18,3584]{1,0:T(8,128)(2,1)} %param.27) | copy-start | bytes 387076
  192.2 75.9 %copy-start.6 = (f32[3584]{0:T(1024)S(1)}, f32[3584]{0:T(1024)}, u32[]{:S(2)}) copy-start(f32[3584]{0:T(1024)} %param.26) | copy-start | bytes 43012
  192.2 109.4 %all-gather.5.cloned.1.call-start = ((), (), s32[]{:S(2)}) async-start(), calls=%async_computation.1 | async-start | bytes 2580480 | tf_op jit(solution)/shard_map/all_gather | solution.py:74
Sparse Core Ops, SparseCore 0:
  48.7 110.4 all-reduce.3
  161.6 63.5 all-gather.2
  227.5 39.3 all-reduce.5
  268.4 33.0 all-gather.4
where the time goes:
time: 382 us
  blocking collectives  190 us (50%)
  waiting for transfers between devices  99.3 us (26%)
  matrix products  43.3 us (11%)
  local copies, waits for them, and re-layouts  27.5 us (7%)
  between operations  16 us (4%)
  other arithmetic  5.25 us (1%)
    psum x1, blocking collectives, per_device(): summed = lax.psum((numer, denom), 'blk')  125 us
    psum x1, blocking collectives, per_device(): totals, picked = lax.psum((totals, picked), ('blk', 'mp'))  64.9 us
    psum x1, waiting for transfers between devices, per_device(): lax.psum(jnp.dot(heads_out, out_weight, preferred_element_type=jnp.float3...  34.1 us
    all_gather x1, waiting for transfers between devices, per_device(): lax.all_gather(medusa_w, 'blk', axis=1, tiled=True)  32.7 us
    all_gather x1, waiting for transfers between devices, per_device(): full_fresh = lax.all_gather(fresh, 'mp', axis=2, tiled=True)  31.7 us
    dot_general x2, matrix products, attend(): jnp.einsum('qhrd,khd->hrqk', query_view, key_view, preferred_element_type...  11.3 us
    dot_general x2, matrix products, attend(): jnp.einsum('hrqk,khd->qhrd', weights.astype(jnp.bfloat16), value_view, pr...  9.63 us
    unnamed x19, local copies, waits for them, and re-layouts  7.84 us
  transfers between devices with their start and end apart: 4, of which 3 were waited for; matrix products, arithmetic and copies ran while one was open for 7% of the time, Pallas kernels for 0%

commit v1 on v0

--- a/solution.py
+++ b/solution.py
@@ -4,6 +4,7 @@
 from jax.sharding import PartitionSpec as P
 
 HEAD_SIZE = 256
+spread_figure_over_axis = lambda inp: lax.psum(lax.psum(inp, axis_name="mp"), axis_name="blk")
 
 
 def capped(values, limit):
@@ -81,7 +82,7 @@
     local_ids = cand_ids - first_id
     match = local_ids[..., None] == jnp.arange(vocab_dev, dtype=jnp.int32)
     picked = jnp.sum(jnp.where(match, logits[:, :, None, :], 0.0), -1)
-    totals, picked = lax.psum((totals, picked), ("blk", "mp"))
+    totals, picked = spread_figure_over_axis((totals, picked))
     draft_logprob = picked - jnp.log(totals)[..., None]
     groups, tree_size, features = tree_q.shape
     keys = prompt_key_value[0, 0]

time: 382 us -> 341 us (0.89)
  blocking collectives: 190 us -> 136 us
  other arithmetic: 5.25 us -> 9.69 us
    psum x2, blocking collectives: 190 us -> 136 us  [the longest x1 122 us: lax.psum(lax.psum(inp, axis_name='mp'), axis_name='blk')]
    all_gather x1, waiting for transfers between devices: 31.7 us -> 0.01 us  [per_device(): full_fresh = lax.all_gather(fresh, 'mp', axis=2, tiled=True)]
    all_gather x1, waiting for transfers between devices: 32.7 us -> 61.9 us  [per_device(): lax.all_gather(medusa_w, 'blk', axis=1, tiled=True)]
    psum x1, waiting for transfers between devices: 34.1 us -> 39 us  [per_device(): lax.psum(jnp.dot(heads_out, out_weight, preferred_element_type=jnp.float3...]
    unnamed x19 -> x23, local copies, waits for them, and re-layouts: 7.84 us -> 8.09 us
  transfers between devices with their start and end apart: 4 -> 4, of which waited for: 3 -> 2; matrix products, arithmetic and copies ran while one was open for 7% -> 20% of each run, Pallas kernels for 0% -> 0%
where the time goes in v1:
time: 341 us; the launch traced here: 339 us
  blocking collectives  136 us (40%)
  waiting for transfers between devices  102 us (30%)
  matrix products  45.2 us (13%)
  local copies, waits for them, and re-layouts  29.1 us (9%)
  between operations  16 us (5%)
  other arithmetic  9.69 us (3%)
    psum x1, blocking collectives, lax.psum(lax.psum(inp, axis_name='mp'), axis_name='blk')  122 us
    all_gather x1, waiting for transfers between devices, per_device(): lax.all_gather(medusa_w, 'blk', axis=1, tiled=True)  61.9 us
    psum x1, waiting for transfers between devices, per_device(): lax.psum(jnp.dot(heads_out, out_weight, preferred_element_type=jnp.float3...  39 us
    psum x1, blocking collectives, lax.psum(inp, axis_name='mp')  14.1 us
    dot_general x2, matrix products, attend(): jnp.einsum('qhrd,khd->hrqk', query_view, key_view, preferred_element_type...  13.1 us
    dot_general x2, matrix products, attend(): jnp.einsum('hrqk,khd->qhrd', weights.astype(jnp.bfloat16), value_view, pr...  9.6 us
    unnamed x23, local copies, waits for them, and re-layouts  8.09 us
    dot_general x1, matrix products, per_device(): jnp.einsum('rd,mdu->mru', hidden, lax.all_gather(medusa_w, 'blk', axis=1,...  7.56 us
  transfers between devices with their start and end apart: 4, of which 2 were waited for; matrix products, arithmetic and copies ran while one was open for 20% of the time, Pallas kernels for 0%

profile of v1, /device:TPU:1, one launch (start us, length us, event | category | flops | bytes accessed | tf_op | source)
XLA Modules:
  0.0 338.5 jit_solution(17115979084939883729)
XLA Ops:
  7.2 0.7 all-gather.3.cloned.1.call-update
  9.9 1.0 dynamic-slice_convert_fusion
  10.9 4.5 %fusion.51 = (bf16[1,1,2048,512]{3,2,1,0:T(8,128)(2,1)}, bf16[1,1,2048,512]{3,2,1,0:T(8,128)(2,1)}) fusion(bf16[2,1,2048,512]{3,2,1,0:T(8,128)(2,1)} %param.20), kind=kLoop, calls=%fused_computation.70 | loop fusion | bytes 8388608 | tf_op jit(solution)/shard_map/slice | solution.py:89
  15.4 61.9 %all-gather.3.cloned.1.call-done = bf16[2,3584,896]{2,1,0:T(8,128)(2,1)} async-done(((bf16[2,112,896]{2,1,0:T(8,128)(2,1)}), bf16[2,3584,896]{2,1,0:T(8,128)(2,1)}) %all-gather.3.cloned.1.call-update) | async-done | bytes 12845072 | tf_op jit(solution)/shard_map/all_gather | solution.py:68
  77.3 7.6 %add_convert_fusion = bf16[2,144,896]{2,1,0:T(8,128)(2,1)} fusion(bf16[2,3584,896]{2,1,0:T(8,128)(2,1)} %all-gather.3.cloned.1.call-done, bf16[144,3584]{1,0:T(8,128)(2,1)S(1)} %copy-done.5, f32[144,896]{1,0:T(8,128)S(1)} %dynamic-slice_convert_fusion), kind=kOutput, calls=%fused_computation.32 | convolution fusion | flops 1851236352 | bytes 14909440 | tf_op jit(solution)/shard_map/rd,mdu->mru/dot_general | solution.py:65
  84.9 0.2 all-reduce.5.cloned.1.call-start
  85.1 2.5 broadcast_multiply_fusion
  87.6 2.9 copy.79
  90.6 4.0 %reshape_reshape.3 = bf16[576,2,2,256]{3,2,1,0:T(2,128)(2,1)} reshape(bf16[12,48,1024]{2,1,0:T(8,128)(2,1)} %param.18) | data formatting | bytes 2359296 | tf_op jit(solution)/shard_map/reshape;reshape | solution.py:31
  94.6 4.1 %copy.80 = bf16[1,1,2048,512]{2,3,1,0:T(8,128)(2,1)} copy(bf16[1,1,2048,512]{3,2,1,0:T(8,128)(2,1)} %get-tuple-element.9) | data formatting | bytes 4194304
  98.7 12.2 %fusion = (f32[2,2,576]{2,1,0:T(2,128)}, f32[2,2048,576,2]{1,2,3,0:T(8,128)}) fusion(f32[576,2048]{1,0:T(8,128)} %broadcast_multiply_fusion, bf16[2048,2,256,1]{0,2,3,1:T(8,128)(2,1)S(1)} %bitcast.85, bf16[576,2,2,256]{3,2,1,0:T(2,128)(2,1)} %reshape_reshape.3), kind=kOutput, calls=%fused_computation.1 | convolution fusion | flops 2434791168 | bytes 26878976 | tf_op jit(solution)/shard_map/qhrd,khd->hrqk/dot_general | solution.py:34
  110.9 9.1 %fusion.6 = f32[576,2,2,256]{3,0,2,1:T(8,128)S(1)} fusion(bf16[2048,2,256,1]{0,2,3,1:T(8,128)(2,1)S(1)} %bitcast.87, f32[2,2048,576,2]{1,2,3,0:T(8,128)} %get-tuple-element.16, f32[576,2048]{1,0:T(8,128)S(1)} %bitcast.84), kind=kOutput, calls=%fused_computation.10 | convolution fusion | flops 2434793472 | bytes 28049408 | tf_op jit(solution)/shard_map/hrqk,khd->qhrd/dot_general | solution.py:39
  120.0 1.8 copy.56
  121.8 2.9 reshape.101
  124.8 0.3 all-reduce.7.cloned.1.call-start
  125.0 0.6 fusion.40
  125.6 0.4 copy-done
  126.0 0.9 reshape.102
  126.9 0.7 broadcast_subtract_fusion.1
  127.7 0.6 copy.50
  128.3 0.7 reshape.104
  129.0 0.1 fusion.52
  129.1 0.1 reshape_squeeze.14
  129.2 1.4 convolution_minimum_fusion.5
  130.6 0.4 convolution_minimum_fusion.4
  131.1 0.4 convolution_minimum_fusion.3
  131.5 0.4 convolution_minimum_fusion.2
  131.9 0.4 convolution_minimum_fusion.1
  132.3 0.4 convolution_minimum_fusion
  132.8 0.1 copy.59
  132.9 0.9 fusion.53
  133.8 0.1 reshape.105
  133.9 0.1 reshape_squeeze.15
  134.0 0.5 convolution_bitcast_fusion
  134.6 1.8 copy.62
  136.4 2.9 reshape.103
  139.4 6.4 %exponential_reduce_fusion = (f32[2,144]{1,0:T(2,128)S(1)}, f32[2,144,1024]{2,1,0:T(8,128)S(1)}) fusion(bf16[2,144,3584]{2,1,0:T(8,128)(2,1)} %all-gather.5.cloned.1.call-done, bf16[1024,3584]{1,0:T(8,128)(2,1)} %param.16), kind=kOutput, calls=%fused_computation.24 | convolution fusion | flops 2114813696 | bytes 10585216 | tf_op jit(solution)/shard_map/mrd,vd->mrv/dot_general | solution.py:77
  145.7 1.8 select_reduce_fusion
  147.6 14.1 %all-reduce.1 = (f32[2,144,10]{1,2,0:T(8,128)S(1)}, f32[2,144]{1,0:T(2,128)S(1)}) all-reduce(f32[2,144,10]{1,2,0:T(8,128)S(1)} %select_reduce_fusion, f32[2,144]{1,0:T(2,128)S(1)} %get-tuple-element.13), channel_id=1, replica_groups=mesh['blk'=32,'mp'=4] {'mp'}, use_global_device_ids=true, to_apply=%region_1.2 | all-reduce | flops 3168 | bytes 25344 | tf_op jit(solution)/shard_map/psum | solution.py:7
  161.7 122.2 %all-reduce = (f32[2,144,10]{1,2,0:T(8,128)S(1)}, f32[2,144]{1,0:T(2,128)S(1)}, f32[576,4]{0,1:T(4,128)S(1)}) all-reduce(f32[2,144,10]{1,2,0:T(8,128)S(1)} %get-tuple-element.7, f32[2,144]{1,0:T(2,128)S(1)} %get-tuple-element.8, f32[576,4]{0,1:T(4,128)S(1)} %reshape.104), channel_id=1, replica_groups=mesh['blk'=32,'mp'=4] {'blk'}, use_global_device_ids=true, to_apply=%region_2.3 | all-reduce | flops 5472 | bytes 43776 | tf_op jit(solution)/shard_map/psum | solution.py:7
  283.9 0.1 dynamic-slice_add_fusion
  284.0 0.1 copy.64
  284.1 0.1 div.48
  284.3 5.1 %fusion.39 = f32[18,3584]{1,0:T(8,128)} fusion(bf16[1024,3584]{1,0:T(8,128)(2,1)} %param.25, f32[18,1024]{1,0:T(8,128)S(1)} %bitcast.89, f32[576,1024]{1,0:T(8,128)} %reshape.103, s32[]{:T(128)S(6)} %select_n.25, f32[576,1024]{1,0:T(8,128)} %all-reduce.5.cloned.1.call-done), kind=kOutput, calls=%fused_computation.47 | convolution fusion | flops 132175872 | bytes 7868420 | tf_op jit(solution)/shard_map/dot_general | solution.py:119
  289.5 0.6 copy.65
  290.1 39.0 %all-reduce.7.cloned.1.call-done = f32[18,3584]{1,0:T(8,128)} async-done(((f32[18,3584]{1,0:T(8,128)}), f32[18,3584]{1,0:T(8,128)}) %all-reduce.7.cloned.1.call-update) | async-done | bytes 258064 | tf_op jit(solution)/shard_map/psum | solution.py:119
  329.1 1.1 multiply_reduce_fusion
  330.2 1.8 add_convert_fusion.1
  (34 shorter events, 0.3 us)
Async XLA Ops:
  7.2 70.1 %all-gather.3.cloned.1.call-start = ((), (), s32[]{:S(2)}) async-start(), calls=%async_computation | async-start | bytes 13246464 | tf_op jit(solution)/shard_map/all_gather | solution.py:68
  7.9 131.5 %all-gather.5.cloned.1.call-start = ((), (), s32[]{:S(2)}) async-start(), calls=%async_computation.1 | async-start | bytes 2580480 | tf_op jit(solution)/shard_map/all_gather | solution.py:75
  10.9 66.4 %copy-start.5 = (bf16[144,3584]{1,0:T(8,128)(2,1)S(1)}, bf16[144,3584]{1,0:T(8,128)(2,1)}, u32[]{:S(2)}) copy-start(bf16[144,3584]{1,0:T(8,128)(2,1)} %param.14) | copy-start | bytes 3096580
  84.9 199.4 %all-reduce.5.cloned.1.call-start = ((), (), s32[]{:S(2)}) async-start(), calls=%async_computation.2 | async-start | bytes 4718592 | tf_op jit(solution)/shard_map/psum | solution.py:100
  94.6 16.3 %slice-start = ((s8[4718592]{0:T(1024)(128)(4,1)}), s8[524288]{0:T(1024)(128)(4,1)S(1)}, s32[]{:S(2)}) async-start(s8[4718592]{0:T(1024)(128)(4,1)} %bitcast.83), calls=%async_computation.4 | async-start | bytes 1048576
  98.7 12.2 %slice-start.1 = ((s8[4718592]{0:T(1024)(128)(4,1)}), s8[4194304]{0:T(1024)(128)(4,1)S(1)}, s32[]{:S(2)}) async-start(s8[4718592]{0:T(1024)(128)(4,1)} %bitcast.83), calls=%async_computation.5 | async-start | bytes 8388608
  98.7 12.2 %copy-start.1 = (bf16[1,1,2048,512]{2,3,1,0:T(8,128)(2,1)S(1)}, bf16[1,1,2048,512]{2,3,1,0:T(8,128)(2,1)}, u32[]{:S(2)}) copy-start(bf16[1,1,2048,512]{2,3,1,0:T(8,128)(2,1)} %copy.80) | copy-start | bytes 6291460
  124.7 1.3 copy-start
  124.7 4.3 %copy-start.2 = (bf16[2,12,48,512]{3,2,1,0:T(8,128)(2,1)S(1)}, bf16[2,12,48,512]{3,2,1,0:T(8,128)(2,1)}, u32[]{:S(2)}) copy-start(bf16[2,12,48,512]{3,2,1,0:T(8,128)(2,1)} %param.19) | copy-start | bytes 3538948
  124.8 204.3 %all-reduce.7.cloned.1.call-start = ((), (), s32[]{:S(2)}) async-start(), calls=%async_computation.3 | async-start | bytes 688128 | tf_op jit(solution)/shard_map/psum | solution.py:119
  139.3 6.4 %copy-start.4 = (s32[2,144,10]{1,2,0:T(8,128)S(1)}, s32[2,144,10]{1,2,0:T(8,128)}, u32[]{:S(2)}) copy-start(s32[2,144,10]{1,2,0:T(8,128)} %copy.50) | copy-start | bytes 34564
  284.3 45.9 %copy-start.3 = (bf16[18,3584]{1,0:T(8,128)(2,1)S(1)}, bf16[18,3584]{1,0:T(8,128)(2,1)}, u32[]{:S(2)}) copy-start(bf16[18,3584]{1,0:T(8,128)(2,1)} %param.27) | copy-start | bytes 387076
  284.3 45.9 %copy-start.6 = (f32[3584]{0:T(1024)S(1)}, f32[3584]{0:T(1024)}, u32[]{:S(2)}) copy-start(f32[3584]{0:T(1024)} %param.26) | copy-start | bytes 43012
Sparse Core Ops, SparseCore 0:
  10.4 66.8 all-gather.2
  85.0 29.9 all-gather.4
  124.9 106.3 all-reduce.4
  289.5 39.4 all-reduce.6
